TPU v7x, 32 devices: a whole 2x2x4 slice. The times are simulated.
32 devices in a mesh: blk: 8 (over z, y), bins: 4 (over x, core).
Axes of the slice: x: 2, y: 2, z: 4, core: 2. Of those that a mesh axis runs over, the one named last changes fastest.
Arguments:
- density: float32 [128, 32768], P('bins', 'blk'), may hold values from 0.05 to 3
- courant: float32 [128, 32768], P('bins', 'blk'), may hold values from -0.5 to 0.3
- gain_tables: float32 [4, 8, 64, 1024], P('bins'), may hold values from -0.0625 to 0.0625
- sources: int32 [4, 8], P('bins'), may hold values from 0 to 3, as said below
- counts: int32 [4], P('bins'), may hold values from 1 to 8, as said below
- targets: int32 [4, 64], P('bins'), may hold values from 0 to 63, each once within a row
- overflow: int32 [4], replicated, may hold values from 1 to 3, as said below
Outputs:
- updated: float32 [128, 32768], P('bins', 'blk')
Inputs may be any that keep to these rules, and one draw needn't show every extreme that they name: sources[g][0] is g; every other entry of row g lies in max(0, g - 2) to g. counts[0] is 1 and counts[3] is 8. `targets`: each row is a permutation of 0 to 63. overflow[0] is 1; for 0 < g < 3, overflow[g] is g + 1 or g + 2, capped at 3; overflow[3] is 3.
All inputs are finite; a program needn't handle non-finite values.
Results may differ from a plain program's by a relative error of at most 0.0003.
Values sent between devices are 32-bit elements; how exact they have to be, the bound alone decides.
A program may use at most 64 MiB of HBM per device.

v0:
```python
import jax
import jax.numpy as jnp
from jax import lax
from jax.sharding import PartitionSpec as P

BLOCK = 512


RATE = 0.5


def padded_2(cells, sides, width):
    for axis, dim in sides:
        count = lax.axis_size(axis)
        ends = count - 1
        head = lax.slice_in_dim(cells, 0, width, axis=dim)
        tail = lax.slice_in_dim(cells, cells.shape[dim] - width, cells.shape[dim], axis=dim)
        cells = jnp.concatenate(
            [
                lax.ppermute(tail, axis, [(i, (i + 1) % count) for i in range(ends)]),
                cells,
                lax.ppermute(head, axis, [((i + 1) % count, i) for i in range(ends)]),
            ],
            axis=dim,
        )
    return cells


def from_behind(value, axis, steps):
    count = lax.axis_size(axis)
    leading, last = (max(0, -steps), min(count, count - steps))
    return lax.ppermute(value, axis, [(source, source + steps) for source in range(leading, last)])


def minmod(first, second):
    agree = first * second > 0.0
    smaller = jnp.where(first > 0.0, jnp.minimum(first, second), jnp.maximum(first, second))
    return jnp.where(agree, smaller, jnp.zeros_like(first))


def advect(padded, speeds):
    width = padded.shape[1] - 4
    slopes = minmod(padded[:, 1:-1] - padded[:, :-2], padded[:, 2:] - padded[:, 1:-1])
    left_state = padded[:, 1 : width + 2] + 0.5 * slopes[:, 0 : width + 1]
    right_state = padded[:, 2 : width + 3] - 0.5 * slopes[:, 1 : width + 2]
    face_speed = speeds[:, 2 : width + 3]
    face_flux = jnp.where(face_speed > 0.0, face_speed * left_state, face_speed * right_state)
    return padded[:, 2 : width + 2] - (face_flux[:, 1:] - face_flux[:, :-1])


def outer_pairs(own_block, src_block):
    return (own_block[:, None, :] * src_block[None, :, :]).reshape(-1, own_block.shape[1])


def per_device(density, courant, gain_tables, sources, counts, targets, overflow):
    group_bins = density.shape[0]
    cell_count = density.shape[1]
    slot_count = gain_tables.shape[1]
    target_count = gain_tables.shape[2]
    group_count = overflow.shape[0]
    own_group = lax.axis_index("bins")
    own_sources = sources[0]
    own_count = counts[0]
    stacked = jnp.stack([density, courant])
    extended = padded_2(stacked, (("blk", 2),), 2)
    advected = advect(extended[0], extended[1])
    picked = (own_sources[:, None, None] == own_group).astype(jnp.float32) * advected[None]
    for distance in range(1, lax.axis_size("bins") // 2 + 1):
        lower = from_behind(advected, "bins", distance)
        picked = (
            picked
            + (own_sources[:, None, None] == own_group - distance).astype(jnp.float32) * lower[None]
        )
    placement = (targets[0][None, :] == jnp.arange(target_count, dtype=jnp.int32)[:, None]).astype(
        jnp.float32
    )

    def per_block(block_index):
        first_row = block_index * BLOCK
        own_block = lax.dynamic_slice_in_dim(advected, first_row, BLOCK, 1)
        src_blocks = lax.dynamic_slice_in_dim(picked, first_row, BLOCK, 2)
        summed = jnp.zeros((target_count, BLOCK), jnp.float32)
        for slot in range(slot_count):

            def compute_slot(src_block, slot=slot):
                return jnp.dot(
                    gain_tables[0, slot],
                    outer_pairs(own_block, src_block),
                    precision=lax.Precision.HIGHEST,
                )

            def skip_slot(src_block):
                return jnp.zeros((target_count, BLOCK), jnp.float32)

            summed = summed + lax.cond(slot < own_count, compute_slot, skip_slot, src_blocks[slot])
        return jnp.dot(placement, summed, precision=lax.Precision.HIGHEST)

    block_count = cell_count // BLOCK
    blocks = lax.map(per_block, jnp.arange(block_count, dtype=jnp.int32))
    placed = blocks.transpose(1, 0, 2).reshape(target_count, cell_count)
    own_gain = placed[:group_bins]
    spill = placed[group_bins:]
    group_ids = jnp.arange(group_count, dtype=jnp.int32)
    to_me = overflow == own_group
    self_weight = jnp.sum(((group_ids == own_group) & to_me).astype(jnp.float32))
    received = self_weight * spill
    for distance in (1, 2):
        arriving = from_behind(spill, "bins", distance)
        weight = jnp.sum(((group_ids == own_group - distance) & to_me).astype(jnp.float32))
        received = received + weight * arriving
    return advected + RATE * (own_gain + received)


def solution(mesh):
    in_specs = (
        P("bins", "blk"),
        P("bins", "blk"),
        P("bins", None, None, None),
        P("bins", None),
        P("bins"),
        P("bins", None),
        P(),
    )
    out_specs = P("bins", "blk")
    return jax.shard_map(
        per_device, mesh=mesh, in_specs=in_specs, out_specs=out_specs, check_vma=False
    )
```

profile of v0, /device:TPU:7, one launch (start us, length us, event | category | flops | bytes accessed | tf_op | source)
XLA Modules:
  0.0 218.3 jit_solution(1343931562246247351)
XLA Ops:
  0.8 3.1 %collective-permute-start = (f32[2,32,2]{2,1,0:T(8,128)S(1)}, f32[2,32,2]{2,1,0:T(8,128)S(1)}, u32[]{:S(2)}, u32[]{:S(2)}) collective-permute-start(f32[2,32,2]{2,1,0:T(8,128)S(1)} %get-tuple-element.326), channel_id=1, source_target_pairs={{0,4},{4,8},{8,12},{12,16},{16,20},{20,24},{24,28},{1,5},{5,9},{9,... | collective-permute-start | bytes 1544 | tf_op jit(solution)/shard_map/ppermute | solution.py:20
  4.0 2.1 collective-permute-start.1
  7.4 2.1 collective-permute-done.1
  15.8 2.3 %collective-permute-done.2 = f32[32,4096]{1,0:T(8,128)S(1)} collective-permute-done((f32[32,4096]{1,0:T(8,128)}, f32[32,4096]{1,0:T(8,128)S(1)}, u32[]{:S(2)}, u32[]{:S(2)}) %collective-permute-start.2) | collective-permute-done | bytes 524320 | tf_op jit(solution)/shard_map/ppermute | solution.py:32
  18.1 17.7 %collective-permute-done.3 = f32[32,4096]{1,0:T(8,128)S(1)} collective-permute-done((f32[32,4096]{1,0:T(8,128)}, f32[32,4096]{1,0:T(8,128)S(1)}, u32[]{:S(2)}, u32[]{:S(2)}) %collective-permute-start.3) | collective-permute-done | bytes 524320 | tf_op jit(solution)/shard_map/ppermute | solution.py:32
  35.9 3.9 %multiply_add_fusion = f32[8,32,4096]{2,1,0:T(8,128)} fusion(f32[32,4096]{1,0:T(8,128)S(1)} %collective-permute-done.3, f32[8]{0:T(128)S(1)} %get-tuple-element.328, f32[32,4096]{1,0:T(8,128)S(1)} %collective-permute-done.2, f32[8]{0:T(128)S(1)} %get-tuple-element.329, f32[32,4096]{1,0:T(8,128)} %fusion.33, f32[8]{0:T(128)S(1)} %get-tuple-element.327), kind=kLoop, calls=%fused_computation.55 | loop fusion | flops 5242880 | bytes 5767264 | tf_op jit(solution)/shard_map/add | solution.py:71
  39.8 157.7 %while.13 = (s32[]{:T(128)}, f32[8,64,512]{2,1,0:T(8,128)}, pred[]{:T(512)}, s32[8]{0:T(128)S(1)}, f32[32,4096]{1,0:T(8,128)}, /*index=5*/f32[8,32,4096]{2,1,0:T...) while((s32[]{:T(128)}, f32[8,64,512]{2,1,0:T(8,128)}, ...), condition=%wide.region_17.18_spmd.clone, body=%wide.region_0.17_spmd.clone.sunk | while | flops 3250823168 | bytes 41157740 | solution.py:99
  44.8 1.8 conditional.26
  46.6 1.8 conditional.27
  48.3 1.8 conditional.28
  50.1 1.8 conditional.29
  51.9 1.8 conditional.30
  53.6 2.5 %conditional.31 = (f32[64,512]{1,0:T(8,128)}) conditional(s32[]{:T(128)} %convert_element_type.147, () %tuple.109, (f32[32,512]{1,0:T(8,128)S(1)}, f32[8,32,512]{2,1,0:T(8,128)S(1)}, f32[1,8,64,1024]{3,2,1,0:T(8,128)S(1)}) %tuple.102), branch_computations={%region_3.3_spmd, %region_4.4_spmd} | conditional | flops 403177472 | bytes 4849672 | solution.py:95
  53.9 2.2 convolution_bitcast_fusion.1
  57.8 1.9 fusion.55
  64.5 1.8 conditional.26
  66.3 1.8 conditional.27
  68.0 1.8 conditional.28
  69.8 1.8 conditional.29
  71.6 1.8 conditional.30
  73.3 2.5 %conditional.31 = (f32[64,512]{1,0:T(8,128)}) conditional(s32[]{:T(128)} %convert_element_type.147, () %tuple.109, (f32[32,512]{1,0:T(8,128)S(1)}, f32[8,32,512]{2,1,0:T(8,128)S(1)}, f32[1,8,64,1024]{3,2,1,0:T(8,128)S(1)}) %tuple.102), branch_computations={%region_3.3_spmd, %region_4.4_spmd} | conditional | flops 403177472 | bytes 4849672 | solution.py:95
  73.6 2.2 convolution_bitcast_fusion.1
  77.5 1.9 fusion.55
  93.0 2.5 %conditional.31 = (f32[64,512]{1,0:T(8,128)}) conditional(s32[]{:T(128)} %convert_element_type.147, () %tuple.109, (f32[32,512]{1,0:T(8,128)S(1)}, f32[8,32,512]{2,1,0:T(8,128)S(1)}, f32[1,8,64,1024]{3,2,1,0:T(8,128)S(1)}) %tuple.102), branch_computations={%region_3.3_spmd, %region_4.4_spmd} | conditional | flops 403177472 | bytes 4849672 | solution.py:95
  93.3 2.2 convolution_bitcast_fusion.1
  97.2 1.9 fusion.55
  103.9 1.8 conditional.26
  105.7 1.8 conditional.27
  107.4 1.8 conditional.28
  109.2 1.8 conditional.29
  110.9 1.8 conditional.30
  112.7 2.5 %conditional.31 = (f32[64,512]{1,0:T(8,128)}) conditional(s32[]{:T(128)} %convert_element_type.147, () %tuple.109, (f32[32,512]{1,0:T(8,128)S(1)}, f32[8,32,512]{2,1,0:T(8,128)S(1)}, f32[1,8,64,1024]{3,2,1,0:T(8,128)S(1)}) %tuple.102), branch_computations={%region_3.3_spmd, %region_4.4_spmd} | conditional | flops 403177472 | bytes 4849672 | solution.py:95
  113.0 2.2 convolution_bitcast_fusion.1
  116.9 1.9 fusion.55
  123.6 1.8 conditional.26
  125.4 1.8 conditional.27
  127.1 1.8 conditional.28
  128.9 1.8 conditional.29
  130.6 1.8 conditional.30
  132.4 2.5 %conditional.31 = (f32[64,512]{1,0:T(8,128)}) conditional(s32[]{:T(128)} %convert_element_type.147, () %tuple.109, (f32[32,512]{1,0:T(8,128)S(1)}, f32[8,32,512]{2,1,0:T(8,128)S(1)}, f32[1,8,64,1024]{3,2,1,0:T(8,128)S(1)}) %tuple.102), branch_computations={%region_3.3_spmd, %region_4.4_spmd} | conditional | flops 403177472 | bytes 4849672 | solution.py:95
  132.7 2.2 convolution_bitcast_fusion.1
  136.6 1.9 fusion.55
  143.3 1.8 conditional.26
  145.0 1.8 conditional.27
  146.8 1.8 conditional.28
  148.6 1.8 conditional.29
  150.3 1.8 conditional.30
  152.1 2.5 %conditional.31 = (f32[64,512]{1,0:T(8,128)}) conditional(s32[]{:T(128)} %convert_element_type.147, () %tuple.109, (f32[32,512]{1,0:T(8,128)S(1)}, f32[8,32,512]{2,1,0:T(8,128)S(1)}, f32[1,8,64,1024]{3,2,1,0:T(8,128)S(1)}) %tuple.102), branch_computations={%region_3.3_spmd, %region_4.4_spmd} | conditional | flops 403177472 | bytes 4849672 | solution.py:95
  152.4 2.2 convolution_bitcast_fusion.1
  156.3 1.9 fusion.55
  163.0 1.8 conditional.26
  164.7 1.8 conditional.27
  166.5 1.8 conditional.28
  168.2 1.8 conditional.29
  170.0 1.8 conditional.30
  171.8 2.5 %conditional.31 = (f32[64,512]{1,0:T(8,128)}) conditional(s32[]{:T(128)} %convert_element_type.147, () %tuple.109, (f32[32,512]{1,0:T(8,128)S(1)}, f32[8,32,512]{2,1,0:T(8,128)S(1)}, f32[1,8,64,1024]{3,2,1,0:T(8,128)S(1)}) %tuple.102), branch_computations={%region_3.3_spmd, %region_4.4_spmd} | conditional | flops 403177472 | bytes 4849672 | solution.py:95
  172.1 2.2 convolution_bitcast_fusion.1
  176.0 1.9 fusion.55
  182.6 1.8 conditional.26
  191.4 2.5 %conditional.31 = (f32[64,512]{1,0:T(8,128)}) conditional(s32[]{:T(128)} %convert_element_type.147, () %tuple.109, (f32[32,512]{1,0:T(8,128)S(1)}, f32[8,32,512]{2,1,0:T(8,128)S(1)}, f32[1,8,64,1024]{3,2,1,0:T(8,128)S(1)}) %tuple.102), branch_computations={%region_3.3_spmd, %region_4.4_spmd} | conditional | flops 403177472 | bytes 4849672 | solution.py:95
  191.7 2.2 convolution_bitcast_fusion.1
  195.6 1.9 fusion.55
  202.7 11.7 %collective-permute-done.5 = f32[32,4096]{1,0:T(8,128)S(1)} collective-permute-done((f32[32,4096]{1,0:T(8,128)S(1)}, f32[32,4096]{1,0:T(8,128)S(1)}, u32[]{:S(2)}, u32[]{:S(2)}) %collective-permute-start.5) | collective-permute-done | bytes 524320 | tf_op jit(solution)/shard_map/ppermute | solution.py:32
  214.4 3.8 %multiply_add_fusion.1 = f32[32,4096]{1,0:T(8,128)} fusion(f32[32,4096]{1,0:T(8,128)} %fusion.33, f32[32,4096]{1,0:T(8,128)S(1)} %bitcast.122, f32[32,4096]{1,0:T(8,128)S(1)} %collective-permute-done.5, f32[32,4096]{1,0:T(8,128)S(1)} %collective-permute-done.4, f32[32,4096]{1,0:T(8,128)S(1)} %bitcast.121, f32[]{:T(128)} %get-tuple-element.289, ...), kind=kLoop, calls=%fused_computation.78 | loop fusion | flops 1048576 | bytes 3145740 | tf_op jit(solution)/shard_map/add | solution.py:111
  (261 shorter events, 174.9 us)
Async XLA Ops:
  0.8 6.6 %collective-permute-start = (f32[2,32,2]{2,1,0:T(8,128)S(1)}, f32[2,32,2]{2,1,0:T(8,128)S(1)}, u32[]{:S(2)}, u32[]{:S(2)}) collective-permute-start(f32[2,32,2]{2,1,0:T(8,128)S(1)} %get-tuple-element.326), channel_id=1, source_target_pairs={{0,4},{4,8},{8,12},{12,16},{16,20},{20,24},{24,28},{1,5},{5,9},{9,... | collective-permute-start | bytes 1544 | tf_op jit(solution)/shard_map/ppermute | solution.py:20
  4.0 5.6 %collective-permute-start.1 = (f32[2,32,2]{2,1,0:T(8,128)S(1)}, f32[2,32,2]{2,1,0:T(8,128)S(1)}, u32[]{:S(2)}, u32[]{:S(2)}) collective-permute-start(f32[2,32,2]{2,1,0:T(8,128)S(1)} %get-tuple-element.325), channel_id=1, source_target_pairs={{4,0},{8,4},{12,8},{16,12},{20,16},{24,20},{28,24},{5,1},{9,5},{13... | collective-permute-start | bytes 1544 | tf_op jit(solution)/shard_map/ppermute | solution.py:22
  10.7 5.0 %copy-start.2 = (s32[1,8]{1,0:T(1,128)S(1)}, s32[1,8]{1,0:T(1,128)}, u32[]{:S(2)}) copy-start(s32[1,8]{1,0:T(1,128)} %param.28) | copy-start | bytes 100
  12.5 5.6 %collective-permute-start.2 = (f32[32,4096]{1,0:T(8,128)}, f32[32,4096]{1,0:T(8,128)S(1)}, u32[]{:S(2)}, u32[]{:S(2)}) collective-permute-start(f32[32,4096]{1,0:T(8,128)} %fusion.33), channel_id=1, source_target_pairs={{0,1},{1,2},{2,3},{4,5},{5,6},{6,7},{8,9},{9,10},{10,11},{12,13},{... | collective-permute-start | bytes 1572872 | tf_op jit(solution)/shard_map/ppermute | solution.py:32
  13.8 22.1 %collective-permute-start.3 = (f32[32,4096]{1,0:T(8,128)}, f32[32,4096]{1,0:T(8,128)S(1)}, u32[]{:S(2)}, u32[]{:S(2)}) collective-permute-start(f32[32,4096]{1,0:T(8,128)} %fusion.33), channel_id=1, source_target_pairs={{0,2},{1,3},{4,6},{5,7},{8,10},{9,11},{12,14},{13,15},{16,18},{17,... | collective-permute-start | bytes 1572872 | tf_op jit(solution)/shard_map/ppermute | solution.py:32
  35.9 3.9 %copy-start = (f32[1,8,64,1024]{3,2,1,0:T(8,128)S(1)}, f32[1,8,64,1024]{3,2,1,0:T(8,128)}, u32[]{:S(2)}) copy-start(f32[1,8,64,1024]{3,2,1,0:T(8,128)} %param.27) | copy-start | bytes 6291460
  35.9 3.9 %copy-start.1 = (s32[1,64]{1,0:T(1,128)S(1)}, s32[1,64]{1,0:T(1,128)}, u32[]{:S(2)}) copy-start(s32[1,64]{1,0:T(1,128)} %param.30) | copy-start | bytes 772
  197.5 4.0 %copy-start.3 = (s32[4]{0:T(128)S(1)}, s32[4]{0:T(128)}, u32[]{:S(2)}) copy-start(s32[4]{0:T(128)} %param.31) | copy-start | bytes 52
  198.9 3.8 %collective-permute-start.4 = (f32[32,4096]{1,0:T(8,128)S(1)}, f32[32,4096]{1,0:T(8,128)S(1)}, u32[]{:S(2)}, u32[]{:S(2)}) collective-permute-start(f32[32,4096]{1,0:T(8,128)S(1)} %bitcast.119), channel_id=1, source_target_pairs={{0,1},{1,2},{2,3},{4,5},{5,6},{6,7},{8,9},{9,10},{10,11},{12,13},{... | collective-permute-start | bytes 1572872 | tf_op jit(solution)/shard_map/ppermute | solution.py:32
  200.2 14.2 %collective-permute-start.5 = (f32[32,4096]{1,0:T(8,128)S(1)}, f32[32,4096]{1,0:T(8,128)S(1)}, u32[]{:S(2)}, u32[]{:S(2)}) collective-permute-start(f32[32,4096]{1,0:T(8,128)S(1)} %bitcast.120), channel_id=1, source_target_pairs={{0,2},{1,3},{4,6},{5,7},{8,10},{9,11},{12,14},{13,15},{16,18},{17,... | collective-permute-start | bytes 1572872 | tf_op jit(solution)/shard_map/ppermute | solution.py:32
where the time goes:
time: 222 us; the launch traced here: 218 us
  matrix products  114 us (51%)
  waiting for transfers between devices  34.4 us (15%)
  other arithmetic  28.9 us (13%)
  local copies, waits for them, and re-layouts  22.7 us (10%)
  starting transfers between devices  10.4 us (5%)
  loops' own time  6.91 us (3%)
    dot_general x64, matrix products, compute_slot(): jnp.dot(gain_tables[0, slot], outer_pairs(own_block, src_block), precisio...  99 us
    ppermute x4, waiting for transfers between devices, from_behind(): lax.ppermute(value, axis, [(source, source + steps) for source in range(l...  32.3 us
    mul x64, other arithmetic, outer_pairs(): own_block[:, None, :] * src_block[None, :, :]  16.3 us
    dot_general x8, matrix products, per_block(): return jnp.dot(placement, summed, precision=lax.Precision.HIGHEST)  15 us
    dynamic_slice x8, local copies, waits for them, and re-layouts, per_block(): src_blocks = lax.dynamic_slice_in_dim(picked, first_row, BLOCK, 2)  8.65 us
    dynamic_slice x8, local copies, waits for them, and re-layouts, per_block(): own_block = lax.dynamic_slice_in_dim(advected, first_row, BLOCK, 1)  6.82 us
    ppermute x4, starting transfers between devices, from_behind(): lax.ppermute(value, axis, [(source, source + steps) for source in range(l...  5.16 us
    another operation x1, loops' own time, per_device(): blocks = lax.map(per_block, jnp.arange(block_count, dtype=jnp.int32))  5.07 us
  transfers between devices with their start and end apart: 6, of which 5 were waited for; matrix products, arithmetic and copies ran while one was open for 1% of the time, Pallas kernels for 0%

commit v1 on v0

v1 whole, which is shorter than its diff:
```python
import functools

import jax
import jax.numpy as jnp
from jax import lax
from jax.experimental import pallas as pl
from jax.experimental.pallas import tpu as pltpu
from jax.sharding import PartitionSpec as P

RATE = 0.5
EDGE = 128
CHUNK = 512
HALF = 256
MESH = pl.DeviceIdType.MESH


def minmod(first, second):
    agree = first * second > 0.0
    smaller = jnp.where(first > 0.0, jnp.minimum(first, second), jnp.maximum(first, second))
    return jnp.where(agree, smaller, jnp.zeros_like(first))


def advect_window(cells, speeds):
    width = cells.shape[1]
    diff = cells - pltpu.roll(cells, 1, 1)
    slopes = minmod(diff, pltpu.roll(diff, width - 1, 1))
    left_state = pltpu.roll(cells + 0.5 * slopes, 1, 1)
    right_state = cells - 0.5 * slopes
    flux = jnp.where(speeds > 0.0, speeds * left_state, speeds * right_state)
    moved = cells - (pltpu.roll(flux, width - 1, 1) - flux)
    return moved[:, EDGE : width - EDGE]


def kernel(
    span, group_count, blk_count,
    density, courant, tables, sources, counts, targets, overflow,
    out,
    dpad, upad, tab, adv, spill, parts, lmat,
    load_sem, halo_send, halo_recv, direct_sem, sib_sem, adv_recv,
    sdirect_sem, ssib_sem, spill_recv,
):
    g = lax.axis_index("bins")
    b = lax.axis_index("blk")
    rows, width = density.shape
    chunks = width // CHUNK
    slots = tables.shape[1]
    target_count = tables.shape[2]
    reach = span + 1
    even = lax.rem(g, 2) == 0
    has_left, has_right = b > 0, b < blk_count - 1

    loads = [
        pltpu.make_async_copy(density, dpad.at[:, pl.ds(EDGE, width)], load_sem.at[0]),
        pltpu.make_async_copy(courant, upad.at[:, pl.ds(EDGE, width)], load_sem.at[1]),
        pltpu.make_async_copy(tables.at[0], tab, load_sem.at[2]),
    ]
    for load in loads:
        load.start()

    barrier = pltpu.get_barrier_semaphore()
    expected = jnp.int32(0)
    for step in [s for s in range(-span, span + 1) if s != 0]:
        there = (g + step >= 0) & (g + step < group_count)
        expected = expected + there.astype(jnp.int32)

        @pl.when(there)
        def _():
            pl.semaphore_signal(barrier, inc=1, device_id={"bins": g + step}, device_id_type=MESH)

    for step, there in ((-1, has_left), (1, has_right)):
        expected = expected + there.astype(jnp.int32)

        @pl.when(there)
        def _():
            pl.semaphore_signal(barrier, inc=1, device_id={"blk": b + step}, device_id_type=MESH)

    zero_edge = jnp.zeros((rows, EDGE), jnp.float32)
    upad[:, pl.ds(0, EDGE)] = zero_edge

    @pl.when(jnp.logical_not(has_left))
    def _():
        dpad[:, pl.ds(0, EDGE)] = zero_edge

    @pl.when(jnp.logical_not(has_right))
    def _():
        dpad[:, pl.ds(EDGE + width, EDGE)] = zero_edge
        upad[:, pl.ds(EDGE + width, EDGE)] = zero_edge

    for distance in range(1, reach):

        @pl.when(g < distance)
        def _():
            adv[distance] = jnp.zeros((rows, width), jnp.float32)

    pl.semaphore_wait(barrier, expected)

    def remote(src, dst, send, recv, where):
        return pltpu.make_async_remote_copy(
            src_ref=src, dst_ref=dst, send_sem=send, recv_sem=recv,
            device_id=where, device_id_type=MESH,
        )

    to_right = remote(
        density.at[:, pl.ds(width - EDGE, EDGE)], dpad.at[:, pl.ds(0, EDGE)],
        halo_send.at[0], halo_recv.at[0], {"blk": b + 1},
    )
    to_left = remote(
        density.at[:, pl.ds(0, EDGE)], dpad.at[:, pl.ds(EDGE + width, EDGE)],
        halo_send.at[1], halo_recv.at[1], {"blk": b - 1},
    )
    speed_left = remote(
        courant.at[:, pl.ds(0, EDGE)], upad.at[:, pl.ds(EDGE + width, EDGE)],
        halo_send.at[2], halo_recv.at[2], {"blk": b - 1},
    )

    @pl.when(has_right)
    def _():
        to_right.start()

    @pl.when(has_left)
    def _():
        to_left.start()
        speed_left.start()

    def window(k):
        return pl.ds(pl.multiple_of(k * CHUNK, CHUNK), CHUNK)

    def adv_direct(distance, k):
        return remote(
            adv.at[0, :, window(k)], adv.at[distance, :, window(k)],
            direct_sem.at[distance - 1, k], adv_recv.at[distance - 1, k], {"bins": g + distance},
        )

    def adv_sib(distance, k):
        return remote(
            adv.at[distance - 1, :, window(k)], adv.at[distance, :, window(k)],
            sib_sem.at[distance - 1, k], adv_recv.at[distance - 1, k], {"bins": g + 1},
        )

    def spill_direct(distance, k):
        return remote(
            spill.at[0, :, window(k)], spill.at[distance, :, window(k)],
            sdirect_sem.at[distance - 1, k], spill_recv.at[distance - 1, k], {"bins": g + distance},
        )

    def spill_sib(distance, k):
        return remote(
            spill.at[distance - 1, :, window(k)], spill.at[distance, :, window(k)],
            ssib_sem.at[distance - 1, k], spill_recv.at[distance - 1, k], {"bins": g + 1},
        )

    def sends_direct(distance):
        target = g + distance
        return (target < group_count) & (lax.rem(target, 2) == 0)

    def sends_sib(distance):
        return even & (g + 1 < group_count) & (g >= distance - 1)

    def spills_direct(distance):
        target = g + distance
        fits = (target < group_count) & (lax.rem(target, 2) == 0)
        return fits & (g > 0) if distance > 1 else fits

    def spills_sib(distance):
        fits = even & (g + 1 < group_count)
        return fits & (g > 1) if distance > 1 else fits

    def spill_arrives(distance):
        return g >= (1 if distance == 1 else 3)

    loads[0].wait()
    loads[1].wait()

    @pl.loop(0, chunks)
    def _(c):
        k = lax.rem(c + 1, chunks)

        @pl.when(c == chunks - 2)
        def _():
            @pl.when(has_left)
            def _():
                to_right.wait_recv()

            @pl.when(has_right)
            def _():
                to_left.wait_recv()
                speed_left.wait_recv()

        padded = pl.ds(pl.multiple_of(k * CHUNK, CHUNK), CHUNK + 2 * EDGE)
        adv[0, :, window(k)] = advect_window(dpad[:, padded], upad[:, padded])
        for distance in range(1, reach):

            @pl.when(sends_direct(distance))
            def _():
                adv_direct(distance, k).start()

        @pl.when(sends_sib(1))
        def _():
            adv_sib(1, k).start()

    loads[2].wait()
    place = (
        lax.broadcasted_iota(jnp.int32, (target_count, target_count), 0) == targets[...]
    ).astype(jnp.float32).astype(jnp.bfloat16)
    weights = [
        [
            jnp.where((sources[0, slot] == g - distance) & (slot < counts[0]), 1.0, 0.0)
            for slot in range(slots)
        ]
        for distance in range(reach)
    ]
    pair_count = tab.shape[2]

    @pl.loop(0, pair_count // HALF)
    def _(m):
        columns = pl.ds(pl.multiple_of(m * HALF, HALF), HALF)
        for distance in range(reach):
            table = weights[distance][0] * tab[0, :, columns]
            for slot in range(1, slots):
                table = table + weights[distance][slot] * tab[slot, :, columns]
            high = table.astype(jnp.bfloat16)
            low = (table - high.astype(jnp.float32)).astype(jnp.bfloat16)
            parts[0, distance, :, columns] = jnp.dot(place, high, preferred_element_type=jnp.float32)
            parts[1, distance, :, columns] = jnp.dot(place, low, preferred_element_type=jnp.float32)

    per_tile = EDGE // rows
    pieces = [(part, distance) for part in (0, 1, 0) for distance in range(reach)]
    lane_group = lax.broadcasted_iota(jnp.int32, (target_count, EDGE), 1) // rows

    @pl.loop(0, pair_count // EDGE)
    def _(m):
        columns = pl.ds(pl.multiple_of(m * EDGE, EDGE), EDGE)
        for r in range(per_tile):
            first = pl.multiple_of((m * per_tile + r) * target_count, target_count)
            for start in range(0, len(pieces), per_tile):
                group = pieces[start : start + per_tile]
                tile = None
                for place_at, (part, distance) in enumerate(group):
                    piece = parts[part, distance, :, columns]
                    shift = (place_at - r) * rows % EDGE
                    if shift:
                        piece = pltpu.roll(piece, shift, 1)
                    tile = piece if tile is None else jnp.where(lane_group == place_at, piece, tile)
                used = len(group) * rows
                lmat[pl.ds(first, target_count), pl.ds(start * rows, used)] = tile[:, :used].astype(
                    jnp.bfloat16
                )

    self_weight = jnp.float32(0.0)
    spill_weights = []
    for group in range(group_count):
        self_weight = self_weight + jnp.where((g == group) & (overflow[group] == g), 1.0, 0.0)
    for distance in (1, 2):
        weight = jnp.float32(0.0)
        for group in range(group_count):
            weight = weight + jnp.where((g - distance == group) & (overflow[group] == g), 1.0, 0.0)
        spill_weights.append(RATE * weight)

    block_rows = 4
    @pl.loop(0, chunks)
    def _(c):
        k = lax.rem(c + 1, chunks)
        for distance in range(1, reach):

            @pl.when(g >= distance)
            def _():
                adv_direct(distance, k).wait_recv()
                if distance + 1 < reach:

                    @pl.when(sends_sib(distance + 1))
                    def _():
                        adv_sib(distance + 1, k).start()

        for h in range(CHUNK // HALF):
            cells = pl.ds(pl.multiple_of(k * CHUNK + h * HALF, HALF), HALF)
            highs, lows = [], []
            for distance in range(reach):
                value = adv[distance, :, cells]
                high = value.astype(jnp.bfloat16)
                highs.append(high)
                lows.append((value - high.astype(jnp.float32)).astype(jnp.bfloat16))
            stack = jnp.concatenate(highs + highs + lows, axis=0)
            total = jnp.zeros((target_count, HALF), jnp.float32)
            for block in range(rows // block_rows):
                first = block * block_rows * target_count
                partial = jnp.dot(
                    lmat[pl.ds(first, block_rows * target_count), :], stack,
                    preferred_element_type=jnp.float32,
                )
                for r in range(block_rows):
                    own_row = adv[0, pl.ds(block * block_rows + r, 1), cells]
                    total = total + own_row * partial[r * target_count : (r + 1) * target_count]
            spill[0, :, cells] = total[rows:]
            out[:, cells] = adv[0, :, cells] + RATE * (total[:rows] + self_weight * total[rows:])
        for distance in (1, 2):

            @pl.when(spills_direct(distance))
            def _():
                spill_direct(distance, k).start()

        @pl.when(spills_sib(1))
        def _():
            spill_sib(1, k).start()

    @pl.loop(0, chunks)
    def _(c):
        k = lax.rem(c + 1, chunks)
        for distance in (1, 2):

            @pl.when(spill_arrives(distance))
            def _():
                spill_direct(distance, k).wait_recv()
                if distance == 1:

                    @pl.when(spills_sib(2))
                    def _():
                        spill_sib(2, k).start()

                out[:, window(k)] += spill_weights[distance - 1] * spill[distance, :, window(k)]

    @pl.when(has_right)
    def _():
        to_right.wait_send()

    @pl.when(has_left)
    def _():
        to_left.wait_send()
        speed_left.wait_send()

    @pl.loop(0, chunks)
    def _(k):
        for copy, sends, most in (
            (adv_direct, sends_direct, span),
            (adv_sib, sends_sib, span),
            (spill_direct, spills_direct, 2),
            (spill_sib, spills_sib, 2),
        ):
            for distance in range(1, most + 1):

                @pl.when(sends(distance))
                def _():
                    copy(distance, k).wait_send()


def per_device(density, courant, gain_tables, sources, counts, targets, overflow):
    rows, width = density.shape
    slots, target_count, pair_count = gain_tables.shape[1:]
    group_count = overflow.shape[0]
    span = lax.axis_size("bins") // 2
    reach = span + 1
    chunks = width // CHUNK
    anywhere = pl.BlockSpec(memory_space=pl.ANY)
    scalars = pl.BlockSpec(memory_space=pltpu.SMEM)
    vectors = pl.BlockSpec(memory_space=pltpu.VMEM)
    dma = pltpu.SemaphoreType.DMA
    return pl.pallas_call(
        functools.partial(kernel, span, group_count, lax.axis_size("blk")),
        out_shape=jax.ShapeDtypeStruct((rows, width), jnp.float32),
        in_specs=[anywhere, anywhere, anywhere, scalars, scalars, vectors, scalars],
        out_specs=vectors,
        scratch_shapes=[
            pltpu.VMEM((rows, width + 2 * EDGE), jnp.float32),
            pltpu.VMEM((rows, width + 2 * EDGE), jnp.float32),
            pltpu.VMEM((slots, target_count, pair_count), jnp.float32),
            pltpu.VMEM((reach, rows, width), jnp.float32),
            pltpu.VMEM((3, rows, width), jnp.float32),
            pltpu.VMEM((2, reach, target_count, pair_count), jnp.float32),
            pltpu.VMEM((rows * target_count, 3 * reach * rows), jnp.bfloat16),
            dma((3,)), dma((3,)), dma((3,)),
            dma((span, chunks)), dma((span, chunks)), dma((span, chunks)),
            dma((2, chunks)), dma((2, chunks)), dma((2, chunks)),
        ],
        compiler_params=pltpu.CompilerParams(
            collective_id=0, has_side_effects=True, vmem_limit_bytes=48 * 1024 * 1024
        ),
        name="drift_coagulate",
    )(density, courant, gain_tables, sources, counts, targets, overflow)


def solution(mesh):
    in_specs = (
        P("bins", "blk"),
        P("bins", "blk"),
        P("bins", None, None, None),
        P("bins", None),
        P("bins"),
        P("bins", None),
        P(),
    )
    return jax.shard_map(
        per_device, mesh=mesh, in_specs=in_specs, out_specs=P("bins", "blk"), check_vma=False
    )
```

time: 222 us -> 31.3 us (0.14); the launches traced: 218 us -> 30.7 us
  matrix products: 114 us -> 0 us
  waiting for transfers between devices: 34.4 us -> 0 us
  other arithmetic: 28.9 us -> 0 us
  Pallas kernels: 0 us -> 23.6 us
  local copies, waits for them, and re-layouts: 22.7 us -> 6.43 us
  starting transfers between devices: 10.4 us -> 0 us
  loops' own time: 6.91 us -> 0 us
    dot_general x72 -> x0, matrix products: 114 us -> none  [the longest x64 99 us: compute_slot(): jnp.dot(gain_tables[0, slot], outer_pairs(own_block, src_block), precisio...]
    ppermute x6 -> x0, waiting for transfers between devices: 34.4 us -> none  [the longest x4 32.3 us: from_behind(): lax.ppermute(value, axis, [(source, source + steps) for source in range(l...]
    pallas_call x0 -> x1, Pallas kernels: none -> 23.6 us  [per_device(): pl.pallas_call(functools.partial(kernel, span, group_count, lax.axis_size...]
    dynamic_slice x24 -> x0, local copies, waits for them, and re-layouts: 20.2 us -> none  [the longest x8 8.65 us: per_block(): src_blocks = lax.dynamic_slice_in_dim(picked, first_row, BLOCK, 2)]
    mul x64 -> x0, other arithmetic: 16.3 us -> none  [outer_pairs(): own_block[:, None, :] * src_block[None, :, :]]
    ppermute x6 -> x0, starting transfers between devices: 10.4 us -> none  [the longest x4 5.16 us: from_behind(): lax.ppermute(value, axis, [(source, source + steps) for source in range(l...]
    add x2 -> x0, other arithmetic: 7.75 us -> none  [the longest x1 3.91 us: per_device(): picked + (own_sources[:, None, None] == own_group - distance).astype(jnp....]
    another operation x65 -> x0, loops' own time: 6.91 us -> none  [the longest x1 5.07 us: per_device(): blocks = lax.map(per_block, jnp.arange(block_count, dtype=jnp.int32))]
  transfers between devices with their start and end apart: 6 -> 0, of which waited for: 5 -> 0; matrix products, arithmetic and copies ran while one was open for 1% -> 0% of each run, Pallas kernels for 0% -> 0%
where the time goes in v1:
time: 31.3 us; the launch traced here: 30.7 us
  Pallas kernels  23.6 us (75%)
  local copies, waits for them, and re-layouts  6.43 us (21%)
  between operations  0.67 us (2%)
    pallas_call x1, Pallas kernels, per_device(): pl.pallas_call(functools.partial(kernel, span, group_count, lax.axis_size...  23.6 us
    unnamed x13, local copies, waits for them, and re-layouts  6.43 us

profile of v1, /device:TPU:7, one launch (start us, length us, event | category | flops | bytes accessed | tf_op | source)
XLA Modules:
  0.0 30.7 jit_solution(366762244571245355)
XLA Ops:
  0.7 0.0 copy-start
  0.7 1.6 %copy-done = f32[1,8,64,1024]{3,2,1,0:T(8,128)S(1)} copy-done((f32[1,8,64,1024]{3,2,1,0:T(8,128)S(1)}, f32[1,8,64,1024]{3,2,1,0:T(8,128)}, u32[]{:S(2)}) %copy-start) | copy-done | bytes 2097176
  2.2 0.0 copy-start.1
  2.2 1.0 %copy-done.1 = f32[32,4096]{1,0:T(8,128)S(1)} copy-done((f32[32,4096]{1,0:T(8,128)S(1)}, f32[32,4096]{1,0:T(8,128)}, u32[]{:S(2)}) %copy-start.1) | copy-done | bytes 524312
  3.3 0.0 copy-start.2
  3.3 1.0 %copy-done.2 = f32[32,4096]{1,0:T(8,128)S(1)} copy-done((f32[32,4096]{1,0:T(8,128)S(1)}, f32[32,4096]{1,0:T(8,128)}, u32[]{:S(2)}) %copy-start.2) | copy-done | bytes 524312
  4.3 0.0 copy-start.3
  4.3 0.7 %copy-done.3 = s32[1,8]{1,0:T(1,128)S(1)} copy-done((s32[1,8]{1,0:T(1,128)S(1)}, s32[1,8]{1,0:T(1,128)}, u32[]{:S(2)}) %copy-start.3) | copy-done | bytes 56
  5.0 0.0 copy-start.4
  5.0 0.7 %copy-done.4 = s32[1,64]{1,0:T(1,128)S(1)} copy-done((s32[1,64]{1,0:T(1,128)S(1)}, s32[1,64]{1,0:T(1,128)}, u32[]{:S(2)}) %copy-start.4) | copy-done | bytes 280
  5.6 0.0 copy-start.5
  5.6 0.7 %copy-done.5 = s32[4]{0:T(128)S(1)} copy-done((s32[4]{0:T(128)S(1)}, s32[4]{0:T(128)}, u32[]{:S(2)}) %copy-start.5) | copy-done | bytes 40
  6.3 23.6 %drift_coagulate.1 = f32[32,4096]{1,0:T(8,128)S(1)} custom-call(f32[32,4096]{1,0:T(8,128)S(1)} %copy-done.1, f32[32,4096]{1,0:T(8,128)S(1)} %copy-done.2, f32[1,8,64,1024]{3,2,1,0:T(8,128)S(1)} %copy-done, s32[1,8]{1,0:T(1,128)S(1)} %copy-done.3, s32[1]{0:T(128)S(6)} %copy.9.counts, s32[1,64]{1,0:T(1,128)S(1)} %copy-done.4, s32[4]{0:T(128)S(1)} %copy-done.5), custom_call_target="tpu_custom_call" | custom-call | tf_op jit(solution)/shard_map/drift_coagulate/pallas_call | solution.py:356
  29.9 0.8 %copy.10 = f32[32,4096]{1,0:T(8,128)} copy(f32[32,4096]{1,0:T(8,128)S(1)} %drift_coagulate.1) | data formatting | bytes 1048576
Async XLA Ops:
  0.7 1.6 %copy-start = (f32[1,8,64,1024]{3,2,1,0:T(8,128)S(1)}, f32[1,8,64,1024]{3,2,1,0:T(8,128)}, u32[]{:S(2)}) copy-start(f32[1,8,64,1024]{3,2,1,0:T(8,128)} %tables.1) | copy-start | bytes 6291460
  2.2 1.0 %copy-start.1 = (f32[32,4096]{1,0:T(8,128)S(1)}, f32[32,4096]{1,0:T(8,128)}, u32[]{:S(2)}) copy-start(f32[32,4096]{1,0:T(8,128)} %density.1) | copy-start | bytes 1572868
  3.3 1.0 %copy-start.2 = (f32[32,4096]{1,0:T(8,128)S(1)}, f32[32,4096]{1,0:T(8,128)}, u32[]{:S(2)}) copy-start(f32[32,4096]{1,0:T(8,128)} %courant.1) | copy-start | bytes 1572868
  4.3 0.7 %copy-start.3 = (s32[1,8]{1,0:T(1,128)S(1)}, s32[1,8]{1,0:T(1,128)}, u32[]{:S(2)}) copy-start(s32[1,8]{1,0:T(1,128)} %sources.1) | copy-start | bytes 100
  5.0 0.7 %copy-start.4 = (s32[1,64]{1,0:T(1,128)S(1)}, s32[1,64]{1,0:T(1,128)}, u32[]{:S(2)}) copy-start(s32[1,64]{1,0:T(1,128)} %targets.1) | copy-start | bytes 772
  5.6 0.7 %copy-start.5 = (s32[4]{0:T(128)S(1)}, s32[4]{0:T(128)}, u32[]{:S(2)}) copy-start(s32[4]{0:T(128)} %overflow.1) | copy-start | bytes 52

commit v2 on v1

--- a/solution.py
+++ b/solution.py
@@ -9,7 +9,7 @@
 
 RATE = 0.5
 EDGE = 128
-CHUNK = 512
+CHUNK = 1024
 HALF = 256
 MESH = pl.DeviceIdType.MESH
 
@@ -33,9 +33,9 @@
 
 def kernel(
     span, group_count, blk_count,
-    density, courant, tables, sources, counts, targets, overflow,
+    density, courant, tables, sources_in, counts_in, targets_in, overflow_in,
     out,
-    dpad, upad, tab, adv, spill, parts, lmat,
+    sources, counts, targets, overflow, dpad, upad, tab, adv, spill, parts, lmat, lrest,
     load_sem, halo_send, halo_recv, direct_sem, sib_sem, adv_recv,
     sdirect_sem, ssib_sem, spill_recv,
 ):
@@ -53,6 +53,10 @@
         pltpu.make_async_copy(density, dpad.at[:, pl.ds(EDGE, width)], load_sem.at[0]),
         pltpu.make_async_copy(courant, upad.at[:, pl.ds(EDGE, width)], load_sem.at[1]),
         pltpu.make_async_copy(tables.at[0], tab, load_sem.at[2]),
+        pltpu.make_async_copy(sources_in, sources, load_sem.at[3]),
+        pltpu.make_async_copy(counts_in, counts, load_sem.at[4]),
+        pltpu.make_async_copy(targets_in, targets, load_sem.at[5]),
+        pltpu.make_async_copy(overflow_in, overflow, load_sem.at[6]),
     ]
     for load in loads:
         load.start()
@@ -198,7 +202,8 @@
         def _():
             adv_sib(1, k).start()
 
-    loads[2].wait()
+    for load in loads[2:]:
+        load.wait()
     place = (
         lax.broadcasted_iota(jnp.int32, (target_count, target_count), 0) == targets[...]
     ).astype(jnp.float32).astype(jnp.bfloat16)
@@ -223,8 +228,11 @@
             parts[0, distance, :, columns] = jnp.dot(place, high, preferred_element_type=jnp.float32)
             parts[1, distance, :, columns] = jnp.dot(place, low, preferred_element_type=jnp.float32)
 
+            if distance == span:
+                lrest[:, columns] = parts[0, distance, :, columns].astype(jnp.bfloat16)
+
     per_tile = EDGE // rows
-    pieces = [(part, distance) for part in (0, 1, 0) for distance in range(reach)]
+    pieces = [(part, distance) for part in (0, 1, 0) for distance in range(reach)][:-1]
     lane_group = lax.broadcasted_iota(jnp.int32, (target_count, EDGE), 1) // rows
 
     @pl.loop(0, pair_count // EDGE)
@@ -256,7 +264,7 @@
             weight = weight + jnp.where((g - distance == group) & (overflow[group] == g), 1.0, 0.0)
         spill_weights.append(RATE * weight)
 
-    block_rows = 4
+    block_rows = 8
     @pl.loop(0, chunks)
     def _(c):
         k = lax.rem(c + 1, chunks)
@@ -279,7 +287,8 @@
                 high = value.astype(jnp.bfloat16)
                 highs.append(high)
                 lows.append((value - high.astype(jnp.float32)).astype(jnp.bfloat16))
-            stack = jnp.concatenate(highs + highs + lows, axis=0)
+            stack = jnp.concatenate(highs + highs + lows[:-1], axis=0)
+            last_low = lows[-1].astype(jnp.float32)
             total = jnp.zeros((target_count, HALF), jnp.float32)
             for block in range(rows // block_rows):
                 first = block * block_rows * target_count
@@ -287,9 +296,16 @@
                     lmat[pl.ds(first, block_rows * target_count), :], stack,
                     preferred_element_type=jnp.float32,
                 )
+                outer = []
                 for r in range(block_rows):
                     own_row = adv[0, pl.ds(block * block_rows + r, 1), cells]
                     total = total + own_row * partial[r * target_count : (r + 1) * target_count]
+                    outer.append((own_row * last_low).astype(jnp.bfloat16))
+                pairs = pl.ds(block * block_rows * rows, block_rows * rows)
+                total = total + jnp.dot(
+                    lrest[:, pairs], jnp.concatenate(outer, axis=0),
+                    preferred_element_type=jnp.float32,
+                )
             spill[0, :, cells] = total[rows:]
             out[:, cells] = adv[0, :, cells] + RATE * (total[:rows] + self_weight * total[rows:])
         for distance in (1, 2):
@@ -349,29 +365,33 @@
     span = lax.axis_size("bins") // 2
     reach = span + 1
     chunks = width // CHUNK
-    anywhere = pl.BlockSpec(memory_space=pl.ANY)
-    scalars = pl.BlockSpec(memory_space=pltpu.SMEM)
+    main = pl.BlockSpec(memory_space=pltpu.HBM)
     vectors = pl.BlockSpec(memory_space=pltpu.VMEM)
     dma = pltpu.SemaphoreType.DMA
     return pl.pallas_call(
         functools.partial(kernel, span, group_count, lax.axis_size("blk")),
         out_shape=jax.ShapeDtypeStruct((rows, width), jnp.float32),
-        in_specs=[anywhere, anywhere, anywhere, scalars, scalars, vectors, scalars],
+        in_specs=[main] * 7,
         out_specs=vectors,
         scratch_shapes=[
+            pltpu.SMEM(sources.shape, jnp.int32),
+            pltpu.SMEM(counts.shape, jnp.int32),
+            pltpu.VMEM(targets.shape, jnp.int32),
+            pltpu.SMEM(overflow.shape, jnp.int32),
             pltpu.VMEM((rows, width + 2 * EDGE), jnp.float32),
             pltpu.VMEM((rows, width + 2 * EDGE), jnp.float32),
             pltpu.VMEM((slots, target_count, pair_count), jnp.float32),
             pltpu.VMEM((reach, rows, width), jnp.float32),
             pltpu.VMEM((3, rows, width), jnp.float32),
             pltpu.VMEM((2, reach, target_count, pair_count), jnp.float32),
-            pltpu.VMEM((rows * target_count, 3 * reach * rows), jnp.bfloat16),
-            dma((3,)), dma((3,)), dma((3,)),
+            pltpu.VMEM((rows * target_count, (3 * reach - 1) * rows), jnp.bfloat16),
+            pltpu.VMEM((target_count, pair_count), jnp.bfloat16),
+            dma((7,)), dma((3,)), dma((3,)),
             dma((span, chunks)), dma((span, chunks)), dma((span, chunks)),
             dma((2, chunks)), dma((2, chunks)), dma((2, chunks)),
         ],
         compiler_params=pltpu.CompilerParams(
-            collective_id=0, has_side_effects=True, vmem_limit_bytes=48 * 1024 * 1024
+            collective_id=0, has_side_effects=True, vmem_limit_bytes=67043328
         ),
         name="drift_coagulate",
     )(density, courant, gain_tables, sources, counts, targets, overflow)

time: 31.3 us -> 25.9 us (0.83); the launches traced: 30.7 us -> 25.8 us
  local copies, waits for them, and re-layouts: 6.43 us -> 1.87 us
  Pallas kernels: 23.6 us -> 23.2 us
    unnamed x13 -> x1, local copies, waits for them, and re-layouts: 6.43 us -> 1.87 us
    pallas_call x1, Pallas kernels: 23.6 us -> 23.2 us  [per_device(): pl.pallas_call(functools.partial(kernel, span, group_count, lax.axis_size...]
where the time goes in v2:
time: 25.9 us; the launch traced here: 25.8 us
  Pallas kernels  23.2 us (90%)
  local copies, waits for them, and re-layouts  1.87 us (7%)
  between operations  0.66 us (3%)
    pallas_call x1, Pallas kernels, per_device(): pl.pallas_call(functools.partial(kernel, span, group_count, lax.axis_size...  23.2 us
    unnamed x1, local copies, waits for them, and re-layouts  1.87 us

profile of v2, /device:TPU:7, one launch (start us, length us, event | category | flops | bytes accessed | tf_op | source)
XLA Modules:
  0.0 25.8 jit_solution(13938468128025871409)
XLA Ops:
  0.7 23.2 %drift_coagulate.1 = f32[32,4096]{1,0:T(8,128)} custom-call(f32[32,4096]{1,0:T(8,128)} %density.1, f32[32,4096]{1,0:T(8,128)} %courant.1, f32[1,8,64,1024]{3,2,1,0:T(8,128)} %tables.1, s32[1,8]{1,0:T(1,128)} %sources_in.1, s32[1]{0:T(128)S(6)} %copy.9.counts_in, s32[1,64]{1,0:T(1,128)} %targets_in.1, s32[4]{0:T(128)} %overflow_in.1), custom_call_target="tpu_custom_call" | custom-call | tf_op jit(solution)/shard_map/drift_coagulate/pallas_call | solution.py:371
  23.9 1.9 %copy.10 = f32[32,4096]{1,0:T(8,128)} copy(f32[32,4096]{1,0:T(8,128)} %drift_coagulate.1) | data formatting | bytes 1048576
